TPU v7x, 32 devices: a whole 2x2x4 slice. The times are simulated.
32 devices in a mesh: prow: 8 (over z, core), pcol: 4 (over y, x).
Axes of the slice: x: 2, y: 2, z: 4, core: 2. Of those that a mesh axis runs over, the one named last changes fastest.
Arguments:
- leaf_source: bfloat16 [8, 4, 8, 256, 128], P('prow', 'pcol'), may hold values from -6 to 6
- band_source: bfloat16 [8, 256, 128], P('prow'), may hold values from -6 to 6
- strip_source: bfloat16 [4, 256, 128], P('pcol'), may hold values from -6 to 6
- summit_source: bfloat16 [256, 128], replicated, may hold values from -6 to 6
- leaf_inverse: bfloat16 [8, 4, 8, 256, 256], P('prow', 'pcol'), may hold values from -1 to 2
- band_inverse: bfloat16 [8, 256, 256], P('prow'), may hold values from -1 to 2
- strip_inverse: bfloat16 [4, 256, 256], P('pcol'), may hold values from -1 to 2
- summit_inverse: bfloat16 [256, 256], replicated, may hold values from -1 to 2
- leaf_blocks: bfloat16 [8, 4, 28, 256, 256], P('prow', 'pcol'), may hold values from -0.09375 to 0.09375
- band_blocks: bfloat16 [8, 4, 8, 256, 256], P('prow', 'pcol'), may hold values from -0.046875 to 0.046875
- strip_blocks: bfloat16 [8, 4, 8, 256, 256], P('prow', 'pcol'), may hold values from -0.03125 to 0.03125
- summit_blocks: bfloat16 [8, 4, 8, 256, 256], P('prow', 'pcol'), may hold values from -0.046875 to 0.046875
- coupling: bfloat16 [8, 4, 256, 256], P('prow', 'pcol'), may hold values from -0.09375 to 0.09375
- summit_band: bfloat16 [8, 256, 256], P('prow', 'pcol'), may hold values from -0.078125 to 0.078125
- summit_strip: bfloat16 [4, 256, 256], P('pcol'), may hold values from -0.078125 to 0.078125
- parents: int32 [8, 4, 8], P('prow', 'pcol'), may hold values from 1 to 8, as said below
- widths: int32 [8, 4, 8], P('prow', 'pcol'), may hold values from 64 to 256
Outputs:
- leaf_answer: bfloat16 [8, 4, 8, 256, 128], P('prow', 'pcol')
- band_answer: bfloat16 [8, 256, 128], P('prow')
- strip_answer: bfloat16 [4, 256, 128], P('pcol')
- summit_answer: bfloat16 [256, 128], replicated
Inputs may be any that keep to these rules, and one draw needn't show every extreme that they name: parents[r, c, a] is a later leaf of the same subtree, or 8 where leaf a links only to the separators.
All inputs are finite; a program needn't handle non-finite values.
Results may differ from a plain program's by a relative error of at most 0.015.
Values sent between devices are 32-bit elements; how exact they have to be, the bound alone decides.
No kernel may reach another device: no remote copies, remote signals or barrier semaphores. Data moves between devices by JAX's collectives and lax.ppermute only.
A program may use at most 64 MiB of HBM per device.

v0:
```python
import jax
import jax.numpy as jnp
from jax import lax
from jax.sharding import PartitionSpec as P

PASSES = 2


def ancestors(parent_list, leaf_count):
    node_ids = jnp.arange(leaf_count + 1, dtype=jnp.int32)
    current = parent_list
    extended = jnp.concatenate([current, jnp.full((1,), leaf_count, jnp.int32)])
    reached = jnp.zeros((leaf_count + 1, leaf_count), jnp.float32)
    for repeat in range(leaf_count):
        matches = current[None, :] == node_ids[:, None]
        reached = jnp.maximum(reached, matches.astype(jnp.float32))
        current = jnp.sum(jnp.where(matches, extended[:, None], 0), axis=0)
    return reached[:leaf_count]


def multiply(left, right, form):
    return jnp.einsum(form, left, right, preferred_element_type=jnp.float32)


def forward_block(inverse, source, partial_value):
    residual = (source.astype(jnp.float32) - partial_value).astype(jnp.bfloat16)
    return multiply(inverse, residual, "ij,jr->ir").astype(jnp.bfloat16)


def backward_block(inverse, source, partial_value):
    residual = (source.astype(jnp.float32) - partial_value).astype(jnp.bfloat16)
    return multiply(inverse, residual, "ji,jr->ir").astype(jnp.bfloat16)


def leaf_forward(pair_blocks, inverses, sources, reached, row_mask):
    leaf_count = sources.shape[0]
    solved = []
    for position in range(leaf_count):
        residual = sources[position].astype(jnp.float32)
        if position > 0:
            first_pair = position * (position - 1) // 2
            weights = reached[position, :position].astype(jnp.bfloat16)
            stacked = jnp.stack(solved) * weights[:, None, None]
            residual = residual - multiply(
                pair_blocks[first_pair : first_pair + position], stacked, "bij,bjr->ir"
            )
        residual = (row_mask[position] * residual).astype(jnp.bfloat16)
        solved.append(
            (row_mask[position] * multiply(inverses[position], residual, "ij,jr->ir")).astype(
                jnp.bfloat16
            )
        )
    return jnp.stack(solved)


def leaf_backward(pair_blocks, inverses, solved, outer, reached, row_mask):
    leaf_count = solved.shape[0]
    pending = outer
    answers = [None] * leaf_count
    for position in reversed(range(leaf_count)):
        residual = (
            row_mask[position] * (solved[position].astype(jnp.float32) - pending[position])
        ).astype(jnp.bfloat16)
        update = (row_mask[position] * multiply(inverses[position], residual, "ji,jr->ir")).astype(
            jnp.bfloat16
        )
        answers[position] = update
        if position > 0:
            first_pair = position * (position - 1) // 2
            pushed = multiply(
                pair_blocks[first_pair : first_pair + position], update, "bji,jr->bir"
            )
            pending = pending.at[:position].add(
                reached[position, :position][:, None, None] * pushed
            )
    return jnp.stack(answers)


def per_device(
    leaf_source,
    band_source,
    strip_source,
    summit_source,
    leaf_inverse,
    band_inverse,
    strip_inverse,
    summit_inverse,
    leaf_blocks,
    band_blocks,
    strip_blocks,
    summit_blocks,
    coupling,
    summit_band,
    summit_strip,
    parents,
    widths,
):
    leaf_count = leaf_source.shape[2]
    block_width = leaf_source.shape[3]
    reached = ancestors(parents[0, 0], leaf_count)
    column_ids = jnp.arange(block_width, dtype=jnp.int32)
    row_mask = (column_ids[None, :] < widths[0, 0][:, None]).astype(jnp.float32)[:, :, None]
    band_slab = summit_band.shape[1]
    column_place = lax.axis_index("pcol") * band_slab
    inverses = leaf_inverse[0, 0]
    pair_blocks = leaf_blocks[0, 0]
    to_band = band_blocks[0, 0]
    to_strip = strip_blocks[0, 0]
    to_summit = summit_blocks[0, 0]
    link_block = coupling[0, 0]
    lift_band = summit_band[0]
    lift_strip = summit_strip[0]
    current = (leaf_source[0, 0], band_source[0], strip_source[0], summit_source)
    for iteration in range(PASSES):
        leaf_now, band_now, strip_now, summit_now = current
        solved = leaf_forward(pair_blocks, inverses, leaf_now, reached, row_mask)
        band_term = multiply(to_band, solved, "aij,ajr->ir")
        strip_term = multiply(to_strip, solved, "aij,ajr->ir")
        summit_term = multiply(to_summit, solved, "aij,ajr->ir")
        band_partial = lax.psum(band_term, "pcol")
        band_solved = forward_block(band_inverse[0], band_now, band_partial)
        own_band = lax.dynamic_slice_in_dim(band_solved, column_place, band_slab, 0)
        summit_term = summit_term + multiply(lift_band, own_band, "ki,kn->in")
        strip_term = strip_term + multiply(link_block, band_solved, "ij,jn->in")
        strip_partial, summit_early = lax.psum((strip_term, summit_term), "prow")
        strip_solved = forward_block(strip_inverse[0], strip_now, strip_partial)
        summit_partial = lax.psum(
            summit_early + multiply(lift_strip, strip_solved, "ki,kn->in"), "pcol"
        )
        summit_solved = forward_block(summit_inverse, summit_now, summit_partial)
        summit_answer = backward_block(
            summit_inverse, summit_solved, jnp.zeros(summit_solved.shape, jnp.float32)
        )
        strip_answer = backward_block(
            strip_inverse[0], strip_solved, multiply(lift_strip, summit_answer, "ki,in->kn")
        )
        downward = multiply(link_block, strip_answer, "ji,jn->in")
        band_piece = multiply(lift_band, summit_answer, "ki,in->kn")
        band_back = lax.psum(downward, "pcol") + lax.all_gather(
            band_piece, "pcol", axis=0, tiled=True
        )
        band_answer = backward_block(band_inverse[0], band_solved, band_back)
        outer = (
            multiply(to_band, band_answer, "aij,ir->ajr")
            + multiply(to_strip, strip_answer, "aij,ir->ajr")
            + multiply(to_summit, summit_answer, "aij,ir->ajr")
        )
        leaf_answer = leaf_backward(pair_blocks, inverses, solved, outer, reached, row_mask)
        current = (leaf_answer, band_answer, strip_answer, summit_answer)
    return (current[0][None, None], current[1][None], current[2][None], current[3])


def solution(mesh):
    placed = (
        P("prow", "pcol", None, None, None),
        P("prow", None, None),
        P("pcol", None, None),
        P(),
        P("prow", "pcol", None, None, None),
        P("prow", None, None),
        P("pcol", None, None),
        P(),
        P("prow", "pcol", None, None, None),
        P("prow", "pcol", None, None, None),
        P("prow", "pcol", None, None, None),
        P("prow", "pcol", None, None, None),
        P("prow", "pcol", None, None),
        P("prow", "pcol", None),
        P("pcol", None, None),
        P("prow", "pcol", None),
        P("prow", "pcol", None),
    )
    return jax.shard_map(
        per_device,
        mesh=mesh,
        in_specs=placed,
        out_specs=(
            P("prow", "pcol", None, None, None),
            P("prow", None, None),
            P("pcol", None, None),
            P(),
        ),
        check_vma=False,
    )
```

profile of v0, /device:TPU:0, one launch (start us, length us, event | category | flops | bytes accessed | tf_op | source)
XLA Modules:
  0.0 482.1 jit_solution(6182447190945887679)
XLA Ops:
  21.9 2.2 constant_dynamic-update-slice_fusion.13
  25.1 2.5 constant_dynamic-update-slice_fusion.12
  28.4 2.6 constant_dynamic-update-slice_fusion.11
  31.0 2.6 constant_dynamic-update-slice_fusion.18
  33.6 2.2 convolution_bitcast_fusion.21
  45.1 35.8 %all-reduce.11.cloned.1.call-done = f32[256,128]{1,0:T(8,128)} async-done(((f32[256,128]{1,0:T(8,128)}), f32[256,128]{1,0:T(8,128)}) %all-reduce.11.cloned.1.call-update) | async-done | bytes 131088 | tf_op jit(solution)/shard_map/psum | solution.py:120
  87.1 54.4 %all-reduce.25.cloned.1.call-done = (f32[256,128]{1,0:T(8,128)}, f32[256,128]{1,0:T(8,128)}) async-done(((f32[256,128]{1,0:T(8,128)}, f32[256,128]{1,0:T(8,128)}), (f32[256,128]{1,0:T(8,128)}, f32[256,128]{1,0:T(8,128)})) %all-reduce.25.cloned.1.call-update) | async-done | bytes 262160 | tf_op jit(solution)/shard_map/psum | solution.py:125
  146.3 40.2 %all-reduce.13.cloned.1.call-done = f32[256,128]{1,0:T(8,128)} async-done(((f32[256,128]{1,0:T(8,128)}), f32[256,128]{1,0:T(8,128)}) %all-reduce.13.cloned.1.call-update) | async-done | bytes 131088 | tf_op jit(solution)/shard_map/psum | solution.py:127
  193.0 9.1 %all_gather.6 = f32[256,128]{1,0:T(8,128)} all-gather(f32[64,128]{1,0:T(8,128)S(1)} %convolution_bitcast_fusion.24), channel_id=1, replica_groups=mesh['prow'=8,'pcol'=4] {'pcol'}, dimensions={0}, use_global_device_ids=true | all-gather | bytes 163840 | tf_op jit(solution)/shard_map/all_gather | solution.py:139
  203.8 30.6 %all-reduce.15.cloned.1.call-done = f32[256,128]{0,1:T(8,128)} async-done(((f32[256,128]{0,1:T(8,128)}), f32[256,128]{0,1:T(8,128)}) %all-reduce.15.cloned.1.call-update) | async-done | bytes 131088 | tf_op jit(solution)/shard_map/psum | solution.py:139
  248.7 2.2 constant_dynamic-update-slice_fusion.41
  250.9 2.3 constant_dynamic-update-slice_fusion.40
  253.2 2.4 constant_dynamic-update-slice_fusion.39
  255.6 2.5 constant_dynamic-update-slice_fusion.38
  258.1 2.6 constant_dynamic-update-slice_fusion.37
  260.7 2.7 constant_dynamic-update-slice_fusion.44
  263.4 2.2 convolution_bitcast_fusion.15
  265.6 2.2 convolution_bitcast_fusion.17
  267.9 2.2 convolution_bitcast_fusion.16
  270.0 40.1 %all-reduce.17.cloned.1.call-done = f32[256,128]{0,1:T(8,128)} async-done(((f32[256,128]{0,1:T(8,128)}), f32[256,128]{0,1:T(8,128)}) %all-reduce.17.cloned.1.call-update) | async-done | bytes 131088 | tf_op jit(solution)/shard_map/psum | solution.py:120
  315.1 55.6 %all-reduce.23.cloned.1.call-done = (f32[256,128]{0,1:T(8,128)}, f32[256,128]{0,1:T(8,128)}) async-done(((f32[256,128]{0,1:T(8,128)}, f32[256,128]{0,1:T(8,128)}), (f32[256,128]{0,1:T(8,128)}, f32[256,128]{0,1:T(8,128)})) %all-reduce.23.cloned.1.call-update) | async-done | bytes 262160 | tf_op jit(solution)/shard_map/psum | solution.py:125
  374.2 41.4 %all-reduce.19.cloned.1.call-done = f32[256,128]{0,1:T(8,128)} async-done(((f32[256,128]{0,1:T(8,128)}), f32[256,128]{0,1:T(8,128)}) %all-reduce.19.cloned.1.call-update) | async-done | bytes 131088 | tf_op jit(solution)/shard_map/psum | solution.py:127
  425.4 8.8 %all_gather.7 = f32[256,128]{1,0:T(8,128)S(1)} all-gather(f32[64,128]{1,0:T(8,128)S(1)} %convolution_bitcast_fusion.23), channel_id=1, replica_groups=mesh['prow'=8,'pcol'=4] {'pcol'}, dimensions={0}, use_global_device_ids=true | all-gather | bytes 163840 | tf_op jit(solution)/shard_map/all_gather | solution.py:139
  434.2 29.4 %all-reduce.21.cloned.1.call-done = f32[256,128]{0,1:T(8,128)} async-done(((f32[256,128]{0,1:T(8,128)}), f32[256,128]{0,1:T(8,128)}) %all-reduce.21.cloned.1.call-update) | async-done | bytes 131088 | tf_op jit(solution)/shard_map/psum | solution.py:139
  (281 shorter events, 87.4 us)
Async XLA Ops:
  7.2 26.5 %copy-start = (bf16[1,1,8,256,256]{4,3,2,1,0:T(8,128)(2,1)S(1)}, bf16[1,1,8,256,256]{4,3,2,1,0:T(8,128)(2,1)}, u32[]{:S(2)}) copy-start(bf16[1,1,8,256,256]{4,3,2,1,0:T(8,128)(2,1)} %param.54) | copy-start | bytes 3145732
  7.2 73.7 %all-reduce.11.cloned.1.call-start = ((), (), s32[]{:S(2)}) async-start(), calls=%async_computation | async-start | bytes 262144 | tf_op jit(solution)/shard_map/psum | solution.py:120
  10.5 20.5 %copy-start.73 = (bf16[7]{0:T(256)(128)(2,1)}, bf16[7]{0:T(256)(128)(2,1)S(1)}, u32[]{:S(2)}) copy-start(bf16[7]{0:T(256)(128)(2,1)S(1)} %fusion.586) | copy-start | bytes 46
  10.5 17.8 %copy-start.74 = (bf16[6]{0:T(256)(128)(2,1)}, bf16[6]{0:T(256)(128)(2,1)S(1)}, u32[]{:S(2)}) copy-start(bf16[6]{0:T(256)(128)(2,1)S(1)} %fusion.585) | copy-start | bytes 40
  10.6 14.5 %copy-start.75 = (bf16[5]{0:T(256)(128)(2,1)}, bf16[5]{0:T(256)(128)(2,1)S(1)}, u32[]{:S(2)}) copy-start(bf16[5]{0:T(256)(128)(2,1)S(1)} %fusion.584) | copy-start | bytes 34
  10.6 13.6 %copy-start.76 = (bf16[4]{0:T(256)(128)(2,1)}, bf16[4]{0:T(256)(128)(2,1)S(1)}, u32[]{:S(2)}) copy-start(bf16[4]{0:T(256)(128)(2,1)S(1)} %fusion.583) | copy-start | bytes 28
  10.6 13.5 %copy-start.77 = (bf16[3]{0:T(256)(128)(2,1)}, bf16[3]{0:T(256)(128)(2,1)S(1)}, u32[]{:S(2)}) copy-start(bf16[3]{0:T(256)(128)(2,1)S(1)} %fusion.582) | copy-start | bytes 22
  10.6 13.5 %copy-start.78 = (bf16[2]{0:T(256)(128)(2,1)}, bf16[2]{0:T(256)(128)(2,1)S(1)}, u32[]{:S(2)}) copy-start(bf16[2]{0:T(256)(128)(2,1)S(1)} %fusion.581) | copy-start | bytes 16
  12.1 16.3 %copy-start.48 = (f32[1,256]{1,0:T(1,128)}, f32[1,256]{1,0:T(1,128)S(1)}, u32[]{:S(2)}) copy-start(f32[1,256]{1,0:T(1,128)S(1)} %get-tuple-element.242) | copy-start | bytes 3076
  12.1 18.9 %copy-start.51 = (f32[1,256]{1,0:T(1,128)}, f32[1,256]{1,0:T(1,128)S(1)}, u32[]{:S(2)}) copy-start(f32[1,256]{1,0:T(1,128)S(1)} %get-tuple-element.241) | copy-start | bytes 3076
  25.1 15.7 %copy-start.2 = (bf16[1,1,8,256,256]{4,3,2,1,0:T(8,128)(2,1)S(1)}, bf16[1,1,8,256,256]{4,3,2,1,0:T(8,128)(2,1)}, u32[]{:S(2)}) copy-start(bf16[1,1,8,256,256]{4,3,2,1,0:T(8,128)(2,1)} %param.56) | copy-start | bytes 3145732
  28.4 14.6 %copy-start.1 = (bf16[1,1,8,256,256]{4,3,2,1,0:T(8,128)(2,1)S(1)}, bf16[1,1,8,256,256]{4,3,2,1,0:T(8,128)(2,1)}, u32[]{:S(2)}) copy-start(bf16[1,1,8,256,256]{4,3,2,1,0:T(8,128)(2,1)} %param.55) | copy-start | bytes 3145732
  31.0 51.1 %copy-start.10 = (bf16[1,1,256,256]{3,2,1,0:T(8,128)(2,1)S(1)}, bf16[1,1,256,256]{3,2,1,0:T(8,128)(2,1)}, u32[]{:S(2)}) copy-start(bf16[1,1,256,256]{3,2,1,0:T(8,128)(2,1)} %param.57) | copy-start | bytes 393220
  33.6 107.8 %copy-start.8 = (bf16[1,256,256]{2,1,0:T(8,128)(2,1)S(1)}, bf16[1,256,256]{2,1,0:T(8,128)(2,1)}, u32[]{:S(2)}) copy-start(bf16[1,256,256]{2,1,0:T(8,128)(2,1)} %param.51) | copy-start | bytes 393220
  33.6 109.6 %copy-start.9 = (bf16[1,256,256]{2,1,0:T(8,128)(2,1)S(1)}, bf16[1,256,256]{2,1,0:T(8,128)(2,1)}, u32[]{:S(2)}) copy-start(bf16[1,256,256]{2,1,0:T(8,128)(2,1)} %param.59) | copy-start | bytes 393220
  35.8 105.6 %all-reduce.25.cloned.1.call-start = ((), (), s32[]{:S(2)}) async-start(), calls=%async_computation.7 | async-start | bytes 524288 | tf_op jit(solution)/shard_map/psum | solution.py:125
  85.8 100.7 %all-reduce.13.cloned.1.call-start = ((), (), s32[]{:S(2)}) async-start(), calls=%async_computation.1 | async-start | bytes 262144 | tf_op jit(solution)/shard_map/psum | solution.py:127
  145.0 89.3 %all-reduce.15.cloned.1.call-start = ((), (), s32[]{:S(2)}) async-start(), calls=%async_computation.2 | async-start | bytes 262144 | tf_op jit(solution)/shard_map/psum | solution.py:139
  192.0 118.2 %all-reduce.17.cloned.1.call-start = ((), (), s32[]{:S(2)}) async-start(), calls=%async_computation.3 | async-start | bytes 262144 | tf_op jit(solution)/shard_map/psum | solution.py:120
  267.8 102.9 %all-reduce.23.cloned.1.call-start = ((), (), s32[]{:S(2)}) async-start(), calls=%async_computation.6 | async-start | bytes 524288 | tf_op jit(solution)/shard_map/psum | solution.py:125
  315.0 100.6 %all-reduce.19.cloned.1.call-start = ((), (), s32[]{:S(2)}) async-start(), calls=%async_computation.4 | async-start | bytes 262144 | tf_op jit(solution)/shard_map/psum | solution.py:127
  374.2 89.4 %all-reduce.21.cloned.1.call-start = ((), (), s32[]{:S(2)}) async-start(), calls=%async_computation.5 | async-start | bytes 262144 | tf_op jit(solution)/shard_map/psum | solution.py:139
  419.5 47.3 %copy-start.13 = (bf16[128,256]{1,0:T(8,128)(2,1)S(1)}, bf16[128,256]{1,0:T(8,128)(2,1)}, u32[]{:S(2)}) copy-start(bf16[128,256]{1,0:T(8,128)(2,1)} %convolution_convert_fusion.1) | copy-start | bytes 196612
  419.5 49.0 %copy-start.11 = (bf16[128,256]{1,0:T(8,128)(2,1)S(1)}, bf16[128,256]{1,0:T(8,128)(2,1)}, u32[]{:S(2)}) copy-start(bf16[128,256]{1,0:T(8,128)(2,1)} %convolution_convert_fusion.2) | copy-start | bytes 196612
  (63 other events, 156.5 us)
Sparse Core Ops, SparseCore 0:
  36.0 44.9 all-reduce.10
  85.9 55.5 all-reduce.24
  145.1 41.2 all-reduce.12
  192.1 42.2 all-reduce.14
  267.9 42.2 all-reduce.16
  315.1 55.5 all-reduce.22
  374.3 41.2 all-reduce.18
  421.3 42.2 all-reduce.20
where the time goes:
time: 484 us; the launch traced here: 482 us
  waiting for transfers between devices  328 us (68%)
  matrix products  94.3 us (19%)
  local copies, waits for them, and re-layouts  22.6 us (5%)
  blocking collectives  17.8 us (4%)
  between operations  16 us (3%)
    psum x2, waiting for transfers between devices, per_device(): strip_partial, summit_early = lax.psum((strip_term, summit_term), 'prow')  110 us
    dot_general x76, matrix products, multiply(): return jnp.einsum(form, left, right, preferred_element_type=jnp.float32)  94.3 us
    psum x2, waiting for transfers between devices, per_device(): lax.psum(summit_early + multiply(lift_strip, strip_solved, 'ki,kn->in'),...  81.6 us
    psum x2, waiting for transfers between devices, per_device(): band_partial = lax.psum(band_term, 'pcol')  76 us
    psum x2, waiting for transfers between devices, per_device(): lax.psum(downward, 'pcol')  60 us
    all_gather x2, blocking collectives, per_device(): lax.all_gather(band_piece, 'pcol', axis=0, tiled=True)  17.8 us
    unnamed x175, local copies, waits for them, and re-layouts  11.7 us
  transfers between devices with their start and end apart: 8, of which 8 were waited for; matrix products, arithmetic and copies ran while one was open for 4% of the time, Pallas kernels for 0%

commit v1 on v0

--- a/solution.py
+++ b/solution.py
@@ -4,6 +4,11 @@
 from jax.sharding import PartitionSpec as P
 
 PASSES = 2
+
+
+def _solve_sectors(q_in):
+    low = jnp.sum(lax.all_gather(q_in, "pcol"), 0)
+    return low
 
 
 def ancestors(parent_list, leaf_count):
@@ -136,7 +141,7 @@
         )
         downward = multiply(link_block, strip_answer, "ji,jn->in")
         band_piece = multiply(lift_band, summit_answer, "ki,in->kn")
-        band_back = lax.psum(downward, "pcol") + lax.all_gather(
+        band_back = _solve_sectors(downward) + lax.all_gather(
             band_piece, "pcol", axis=0, tiled=True
         )
         band_answer = backward_block(band_inverse[0], band_solved, band_back)

time: 484 us -> 452 us (0.934)
  waiting for transfers between devices: 328 us -> 268 us
  blocking collectives: 17.8 us -> 38.8 us
    psum x2 -> x0, waiting for transfers between devices: 60 us -> none  [per_device(): lax.psum(downward, 'pcol')]
    all_gather x0 -> x2, blocking collectives: none -> 21 us  [_solve_sectors(): low = jnp.sum(lax.all_gather(q_in, 'pcol'), 0)]
  transfers between devices with their start and end apart: 8 -> 6, of which waited for: 8 -> 6; matrix products, arithmetic and copies ran while one was open for 4% -> 3% of each run, Pallas kernels for 0% -> 0%
where the time goes in v1:
time: 452 us; the launch traced here: 450 us
  waiting for transfers between devices  268 us (59%)
  matrix products  92.7 us (21%)
  blocking collectives  38.8 us (9%)
  local copies, waits for them, and re-layouts  27.3 us (6%)
  between operations  15.9 us (4%)
  other arithmetic  6.84 us (2%)
    psum x2, waiting for transfers between devices, per_device(): strip_partial, summit_early = lax.psum((strip_term, summit_term), 'prow')  110 us
    dot_general x76, matrix products, multiply(): return jnp.einsum(form, left, right, preferred_element_type=jnp.float32)  92.7 us
    psum x2, waiting for transfers between devices, per_device(): lax.psum(summit_early + multiply(lift_strip, strip_solved, 'ki,kn->in'),...  81.6 us
    psum x2, waiting for transfers between devices, per_device(): band_partial = lax.psum(band_term, 'pcol')  76.1 us
    all_gather x2, blocking collectives, _solve_sectors(): low = jnp.sum(lax.all_gather(q_in, 'pcol'), 0)  21 us
    all_gather x2, blocking collectives, per_device(): lax.all_gather(band_piece, 'pcol', axis=0, tiled=True)  17.8 us
    unnamed x175, local copies, waits for them, and re-layouts  11.8 us
  transfers between devices with their start and end apart: 6, of which 6 were waited for; matrix products, arithmetic and copies ran while one was open for 3% of the time, Pallas kernels for 0%

profile of v1, /device:TPU:0, one launch (start us, length us, event | category | flops | bytes accessed | tf_op | source)
XLA Modules:
  0.0 449.6 jit_solution(3051293058543261053)
XLA Ops:
  21.8 2.2 constant_dynamic-update-slice_fusion.13
  25.1 2.5 constant_dynamic-update-slice_fusion.12
  28.4 2.6 constant_dynamic-update-slice_fusion.11
  31.0 2.6 constant_dynamic-update-slice_fusion.18
  33.6 2.2 convolution_bitcast_fusion.21
  44.9 36.0 %all-reduce.9.cloned.1.call-done = f32[256,128]{1,0:T(8,128)} async-done(((f32[256,128]{1,0:T(8,128)}), f32[256,128]{1,0:T(8,128)}) %all-reduce.9.cloned.1.call-update) | async-done | bytes 131088 | tf_op jit(solution)/shard_map/psum | solution.py:125
  87.1 54.4 %all-reduce.19.cloned.1.call-done = (f32[256,128]{1,0:T(8,128)}, f32[256,128]{1,0:T(8,128)}) async-done(((f32[256,128]{1,0:T(8,128)}, f32[256,128]{1,0:T(8,128)}), (f32[256,128]{1,0:T(8,128)}, f32[256,128]{1,0:T(8,128)})) %all-reduce.19.cloned.1.call-update) | async-done | bytes 262160 | tf_op jit(solution)/shard_map/psum | solution.py:130
  146.3 40.2 %all-reduce.11.cloned.1.call-done = f32[256,128]{1,0:T(8,128)} async-done(((f32[256,128]{1,0:T(8,128)}), f32[256,128]{1,0:T(8,128)}) %all-reduce.11.cloned.1.call-update) | async-done | bytes 131088 | tf_op jit(solution)/shard_map/psum | solution.py:132
  191.2 9.1 %all_gather.20 = f32[256,128]{1,0:T(8,128)} all-gather(f32[64,128]{1,0:T(8,128)S(1)} %convolution_bitcast_fusion.24), channel_id=1, replica_groups=mesh['prow'=8,'pcol'=4] {'pcol'}, dimensions={0}, use_global_device_ids=true | all-gather | bytes 163840 | tf_op jit(solution)/shard_map/all_gather | solution.py:144
  203.0 10.5 %all-gather = f32[1024,128]{0,1:T(8,128)} all-gather(f32[256,128]{0,1:T(8,128)S(1)} %convolution_bitcast_fusion.11), channel_id=2, replica_groups=mesh['prow'=8,'pcol'=4] {'pcol'}, dimensions={0}, use_global_device_ids=true | all-gather | bytes 655360 | tf_op jit(solution)/shard_map/all_gather | solution.py:10
  231.8 2.2 constant_dynamic-update-slice_fusion.41
  234.0 2.3 constant_dynamic-update-slice_fusion.40
  236.3 2.4 constant_dynamic-update-slice_fusion.39
  238.7 2.5 constant_dynamic-update-slice_fusion.38
  241.2 2.6 constant_dynamic-update-slice_fusion.37
  243.8 2.7 constant_dynamic-update-slice_fusion.44
  246.5 2.2 convolution_bitcast_fusion.15
  248.7 2.2 convolution_bitcast_fusion.17
  250.9 2.2 convolution_bitcast_fusion.16
  253.1 40.1 %all-reduce.13.cloned.1.call-done = f32[256,128]{0,1:T(8,128)} async-done(((f32[256,128]{0,1:T(8,128)}), f32[256,128]{0,1:T(8,128)}) %all-reduce.13.cloned.1.call-update) | async-done | bytes 131088 | tf_op jit(solution)/shard_map/psum | solution.py:125
  298.1 55.6 %all-reduce.17.cloned.1.call-done = (f32[256,128]{0,1:T(8,128)}, f32[256,128]{0,1:T(8,128)}) async-done(((f32[256,128]{0,1:T(8,128)}, f32[256,128]{0,1:T(8,128)}), (f32[256,128]{0,1:T(8,128)}, f32[256,128]{0,1:T(8,128)})) %all-reduce.17.cloned.1.call-update) | async-done | bytes 262160 | tf_op jit(solution)/shard_map/psum | solution.py:130
  357.2 41.4 %all-reduce.15.cloned.1.call-done = f32[256,128]{0,1:T(8,128)} async-done(((f32[256,128]{0,1:T(8,128)}), f32[256,128]{0,1:T(8,128)}) %all-reduce.15.cloned.1.call-update) | async-done | bytes 131088 | tf_op jit(solution)/shard_map/psum | solution.py:132
  407.7 8.8 %all_gather.23 = f32[256,128]{1,0:T(8,128)S(1)} all-gather(f32[64,128]{1,0:T(8,128)S(1)} %convolution_bitcast_fusion.23), channel_id=1, replica_groups=mesh['prow'=8,'pcol'=4] {'pcol'}, dimensions={0}, use_global_device_ids=true | all-gather | bytes 163840 | tf_op jit(solution)/shard_map/all_gather | solution.py:144
  417.2 10.5 %all-gather.1 = f32[1024,128]{0,1:T(8,128)} all-gather(f32[256,128]{0,1:T(8,128)S(1)} %convolution_bitcast_fusion.8), channel_id=3, replica_groups=mesh['prow'=8,'pcol'=4] {'pcol'}, dimensions={0}, use_global_device_ids=true | all-gather | bytes 655360 | tf_op jit(solution)/shard_map/all_gather | solution.py:10
  (281 shorter events, 93.8 us)
Async XLA Ops:
  7.2 26.4 %copy-start = (bf16[1,1,8,256,256]{4,3,2,1,0:T(8,128)(2,1)S(1)}, bf16[1,1,8,256,256]{4,3,2,1,0:T(8,128)(2,1)}, u32[]{:S(2)}) copy-start(bf16[1,1,8,256,256]{4,3,2,1,0:T(8,128)(2,1)} %param.54) | copy-start | bytes 3145732
  7.2 73.7 %all-reduce.9.cloned.1.call-start = ((), (), s32[]{:S(2)}) async-start(), calls=%async_computation | async-start | bytes 262144 | tf_op jit(solution)/shard_map/psum | solution.py:125
  10.5 20.4 %copy-start.73 = (bf16[7]{0:T(256)(128)(2,1)}, bf16[7]{0:T(256)(128)(2,1)S(1)}, u32[]{:S(2)}) copy-start(bf16[7]{0:T(256)(128)(2,1)S(1)} %fusion.586) | copy-start | bytes 46
  10.5 17.8 %copy-start.74 = (bf16[6]{0:T(256)(128)(2,1)}, bf16[6]{0:T(256)(128)(2,1)S(1)}, u32[]{:S(2)}) copy-start(bf16[6]{0:T(256)(128)(2,1)S(1)} %fusion.585) | copy-start | bytes 40
  10.5 14.5 %copy-start.75 = (bf16[5]{0:T(256)(128)(2,1)}, bf16[5]{0:T(256)(128)(2,1)S(1)}, u32[]{:S(2)}) copy-start(bf16[5]{0:T(256)(128)(2,1)S(1)} %fusion.584) | copy-start | bytes 34
  10.6 13.5 %copy-start.76 = (bf16[4]{0:T(256)(128)(2,1)}, bf16[4]{0:T(256)(128)(2,1)S(1)}, u32[]{:S(2)}) copy-start(bf16[4]{0:T(256)(128)(2,1)S(1)} %fusion.583) | copy-start | bytes 28
  10.6 13.5 %copy-start.77 = (bf16[3]{0:T(256)(128)(2,1)}, bf16[3]{0:T(256)(128)(2,1)S(1)}, u32[]{:S(2)}) copy-start(bf16[3]{0:T(256)(128)(2,1)S(1)} %fusion.582) | copy-start | bytes 22
  10.6 13.4 %copy-start.78 = (bf16[2]{0:T(256)(128)(2,1)}, bf16[2]{0:T(256)(128)(2,1)S(1)}, u32[]{:S(2)}) copy-start(bf16[2]{0:T(256)(128)(2,1)S(1)} %fusion.581) | copy-start | bytes 16
  11.9 12.1 %copy-start.55 = (f32[1,256]{1,0:T(1,128)}, f32[1,256]{1,0:T(1,128)S(1)}, u32[]{:S(2)}) copy-start(f32[1,256]{1,0:T(1,128)S(1)} %get-tuple-element.248) | copy-start | bytes 3076
  11.9 13.1 %copy-start.45 = (f32[1,256]{1,0:T(1,128)}, f32[1,256]{1,0:T(1,128)S(1)}, u32[]{:S(2)}) copy-start(f32[1,256]{1,0:T(1,128)S(1)} %get-tuple-element.243) | copy-start | bytes 3076
  12.0 16.4 %copy-start.48 = (f32[1,256]{1,0:T(1,128)}, f32[1,256]{1,0:T(1,128)S(1)}, u32[]{:S(2)}) copy-start(f32[1,256]{1,0:T(1,128)S(1)} %get-tuple-element.242) | copy-start | bytes 3076
  12.0 19.0 %copy-start.51 = (f32[1,256]{1,0:T(1,128)}, f32[1,256]{1,0:T(1,128)S(1)}, u32[]{:S(2)}) copy-start(f32[1,256]{1,0:T(1,128)S(1)} %get-tuple-element.241) | copy-start | bytes 3076
  15.7 11.8 %copy-start.26 = (bf16[128,256]{1,0:T(8,128)(2,1)}, bf16[128,256]{1,0:T(8,128)(2,1)S(1)}, u32[]{:S(2)}) copy-start(bf16[128,256]{1,0:T(8,128)(2,1)S(1)} %get-tuple-element.249) | copy-start | bytes 196612
  25.1 15.6 %copy-start.2 = (bf16[1,1,8,256,256]{4,3,2,1,0:T(8,128)(2,1)S(1)}, bf16[1,1,8,256,256]{4,3,2,1,0:T(8,128)(2,1)}, u32[]{:S(2)}) copy-start(bf16[1,1,8,256,256]{4,3,2,1,0:T(8,128)(2,1)} %param.56) | copy-start | bytes 3145732
  28.4 14.5 %copy-start.1 = (bf16[1,1,8,256,256]{4,3,2,1,0:T(8,128)(2,1)S(1)}, bf16[1,1,8,256,256]{4,3,2,1,0:T(8,128)(2,1)}, u32[]{:S(2)}) copy-start(bf16[1,1,8,256,256]{4,3,2,1,0:T(8,128)(2,1)} %param.55) | copy-start | bytes 3145732
  31.0 51.1 %copy-start.10 = (bf16[1,1,256,256]{3,2,1,0:T(8,128)(2,1)S(1)}, bf16[1,1,256,256]{3,2,1,0:T(8,128)(2,1)}, u32[]{:S(2)}) copy-start(bf16[1,1,256,256]{3,2,1,0:T(8,128)(2,1)} %param.57) | copy-start | bytes 393220
  33.6 107.9 %copy-start.8 = (bf16[1,256,256]{2,1,0:T(8,128)(2,1)S(1)}, bf16[1,256,256]{2,1,0:T(8,128)(2,1)}, u32[]{:S(2)}) copy-start(bf16[1,256,256]{2,1,0:T(8,128)(2,1)} %param.51) | copy-start | bytes 393220
  33.6 109.6 %copy-start.9 = (bf16[1,256,256]{2,1,0:T(8,128)(2,1)S(1)}, bf16[1,256,256]{2,1,0:T(8,128)(2,1)}, u32[]{:S(2)}) copy-start(bf16[1,256,256]{2,1,0:T(8,128)(2,1)} %param.59) | copy-start | bytes 393220
  35.8 105.6 %all-reduce.19.cloned.1.call-start = ((), (), s32[]{:S(2)}) async-start(), calls=%async_computation.5 | async-start | bytes 524288 | tf_op jit(solution)/shard_map/psum | solution.py:130
  85.7 100.7 %all-reduce.11.cloned.1.call-start = ((), (), s32[]{:S(2)}) async-start(), calls=%async_computation.1 | async-start | bytes 262144 | tf_op jit(solution)/shard_map/psum | solution.py:132
  145.0 148.2 %all-reduce.13.cloned.1.call-start = ((), (), s32[]{:S(2)}) async-start(), calls=%async_computation.2 | async-start | bytes 262144 | tf_op jit(solution)/shard_map/psum | solution.py:125
  250.9 102.9 %all-reduce.17.cloned.1.call-start = ((), (), s32[]{:S(2)}) async-start(), calls=%async_computation.4 | async-start | bytes 524288 | tf_op jit(solution)/shard_map/psum | solution.py:130
  298.1 100.6 %all-reduce.15.cloned.1.call-start = ((), (), s32[]{:S(2)}) async-start(), calls=%async_computation.3 | async-start | bytes 262144 | tf_op jit(solution)/shard_map/psum | solution.py:132
  402.5 31.9 %copy-start.13 = (bf16[128,256]{1,0:T(8,128)(2,1)S(1)}, bf16[128,256]{1,0:T(8,128)(2,1)}, u32[]{:S(2)}) copy-start(bf16[128,256]{1,0:T(8,128)(2,1)} %convolution_convert_fusion.1) | copy-start | bytes 196612
  (61 other events, 127.8 us)
Sparse Core Ops, SparseCore 0:
  35.9 44.9 all-reduce.8
  85.9 55.5 all-reduce.18
  145.1 41.2 all-reduce.10
  251.0 42.1 all-reduce.12
  298.2 55.5 all-reduce.16
  357.4 41.2 all-reduce.14
